TPU v7x, 32 devices: a whole 2x2x4 slice. The times are simulated.
32 devices in a mesh: rows: 16 (over z, x, core), tm: 2 (over y).
Axes of the slice: x: 2, y: 2, z: 4, core: 2. Of those that a mesh axis runs over, the one named last changes fastest.
Arguments:
- patches: bfloat16 [16, 1024, 768], P('rows', 'tm'), may hold values from -6 to 6
- segment_ids: int32 [16, 1024], P('rows', 'tm'), may hold values from 0 to 5, never falling along the last dimension, each value on 1 to 512 neighbouring positions
- mask_positions: int32 [16, 409], P('rows'), may hold values from 0 to 1023, as said below
- mask_embed: bfloat16 [768], replicated, may hold values from -6 to 6
- norm1_gain: bfloat16 [768], replicated, may hold values from 0.5 to 1.5
- norm1_bias: bfloat16 [768], replicated, may hold values from -3 to 3
- w_qkv: bfloat16 [768, 2304], replicated, may hold values from -0.21875 to 0.21875
- query_bias: bfloat16 [768], replicated, may hold values from -3 to 3
- value_bias: bfloat16 [768], replicated, may hold values from -3 to 3
- w_out: bfloat16 [768, 768], replicated, may hold values from -1.75 to 1.75
- out_bias: bfloat16 [768], replicated, may hold values from -3 to 3
- norm2_gain: bfloat16 [768], replicated, may hold values from 0.5 to 1.5
- norm2_bias: bfloat16 [768], replicated, may hold values from -3 to 3
- w_up: bfloat16 [768, 3072], replicated, may hold values from -0.21875 to 0.21875
- up_bias: bfloat16 [3072], replicated, may hold values from -3 to 3
- w_down: bfloat16 [3072, 768], replicated, may hold values from -0.109375 to 0.109375
- down_bias: bfloat16 [768], replicated, may hold values from -3 to 3
- cotangent: bfloat16 [16, 1024, 768], P('rows', 'tm'), may hold values from -6 to 6
Outputs:
- output: bfloat16 [16, 1024, 768], P('rows', 'tm')
- grad_patches: bfloat16 [16, 1024, 768], P('rows', 'tm')
- grad_mask_embed: float32 [768], P('tm')
- grad_norm1_gain: float32 [768], P('tm')
- grad_norm1_bias: float32 [768], P('tm')
- grad_w_qkv: float32 [768, 2304], P('tm')
- grad_query_bias: float32 [768], P('tm')
- grad_value_bias: float32 [768], P('tm')
- grad_w_out: float32 [768, 768], P('tm')
- grad_out_bias: float32 [768], P('tm')
- grad_norm2_gain: float32 [768], P('tm')
- grad_norm2_bias: float32 [768], P('tm')
- grad_w_up: float32 [768, 3072], P('tm')
- grad_up_bias: float32 [3072], P('tm')
- grad_w_down: float32 [3072, 768], P('tm')
- grad_down_bias: float32 [768], P('tm')
Inputs may be any that keep to these rules, and one draw needn't show every extreme that they name: `mask_positions`: the 409 positions of a row are distinct. `segment_ids`: ids never fall along a row; every row has 6 segments.
All inputs are finite; a program needn't handle non-finite values.
Results may differ from a plain program's by a relative error of at most 0.019.
Values may be sent and summed in bfloat16 or wider, within the bound.
A program may use at most 128 MiB of HBM per device.

v0:
```python
from functools import partial
import math

import jax
import jax.numpy as jnp
from jax import lax
from jax.sharding import PartitionSpec as P

HEADS = 12
HEAD = 64


norm_eps = 1e-06
neg_large = -1e30


def normalize(values):
    center = values - jnp.mean(values, axis=-1, keepdims=True)
    scale_inv = lax.rsqrt(jnp.mean(center * center, axis=-1, keepdims=True) + norm_eps)
    return (center * scale_inv, scale_inv)


def norm_back(grad_out, normed, scale_inv, norm_gain):
    grad_normed = grad_out * norm_gain
    mean_one = jnp.mean(grad_normed, axis=-1, keepdims=True)
    mean_two = jnp.mean(grad_normed * normed, axis=-1, keepdims=True)
    return scale_inv * (grad_normed - mean_one - normed * mean_two)


def split_heads(tensor):
    rows_n, length, width = tensor.shape
    return tensor.reshape(rows_n, length, HEADS, width // HEADS).transpose(2, 0, 1, 3)


def join_heads(tensor):
    heads_n, rows_n, length, size = tensor.shape
    return tensor.transpose(1, 2, 0, 3).reshape(rows_n, length, heads_n * size)


def head_scores(query, keys_h, same):
    scores = jnp.einsum("rqd,rkd->rqk", query, keys_h, preferred_element_type=jnp.float32)
    return jnp.where(same, scores, neg_large)


def attend_forward(query_heads, key_heads, value_heads, same):

    def one_head(operands):
        query, keys_h, values_h = operands
        scores = head_scores(query, keys_h, same)
        peak = jnp.max(scores, axis=-1, keepdims=True)
        total = jnp.sum(jnp.exp(scores - peak), axis=-1, keepdims=True)
        log_total = peak + jnp.log(total)
        weights = jnp.exp(scores - log_total).astype(jnp.bfloat16)
        result = jnp.einsum("rqk,rkd->rqd", weights, values_h, preferred_element_type=jnp.float32)
        return (result, log_total[..., 0])

    return lax.map(one_head, (query_heads, key_heads, value_heads))


def attend_backward(query_heads, key_heads, value_heads, grad_heads, log_totals, same):

    def one_head(operands):
        query, keys_h, values_h, grad_out, log_total = operands
        scores = head_scores(query, keys_h, same)
        probs_full = jnp.exp(scores - log_total[..., None])
        probs_low = probs_full.astype(jnp.bfloat16)
        grad_values = jnp.einsum(
            "rqk,rqd->rkd", probs_low, grad_out, preferred_element_type=jnp.float32
        )
        grad_probs = jnp.einsum(
            "rqd,rkd->rqk", grad_out, values_h, preferred_element_type=jnp.float32
        )
        delta = jnp.sum(grad_probs * probs_full, axis=-1, keepdims=True)
        grad_scores = (probs_full * (grad_probs - delta)).astype(jnp.bfloat16)
        grad_query = jnp.einsum(
            "rqk,rkd->rqd", grad_scores, keys_h, preferred_element_type=jnp.float32
        )
        grad_keys = jnp.einsum(
            "rqk,rqd->rkd", grad_scores, query, preferred_element_type=jnp.float32
        )
        return (grad_query, grad_keys, grad_values)

    return lax.map(one_head, (query_heads, key_heads, value_heads, grad_heads, log_totals))


def total_rows(tensor):
    return jnp.sum(tensor.astype(jnp.float32), axis=(0, 1))


def shards(
    patches,
    segment_ids,
    mask_positions,
    mask_embed,
    norm1_gain,
    norm1_bias,
    w_qkv,
    query_bias,
    value_bias,
    w_out,
    out_bias,
    norm2_gain,
    norm2_bias,
    w_up,
    up_bias,
    w_down,
    down_bias,
    cotangent,
):
    rows_n, time_n, width = patches.shape
    query_scale = 1.0 / math.sqrt(HEAD)
    gain_one = norm1_gain.astype(jnp.float32)
    gain_two = norm2_gain.astype(jnp.float32)
    offset = lax.axis_index("tm") * time_n
    places = offset + lax.broadcasted_iota(jnp.int32, (rows_n, time_n, 1), 1)
    masked = jnp.any(places == mask_positions[:, None, :], axis=-1)[..., None]
    inputs = jnp.where(
        masked, mask_embed.astype(jnp.float32)[None, None, :], patches.astype(jnp.float32)
    )
    normed1, inverse1 = normalize(inputs)
    hidden1 = (normed1 * gain_one + norm1_bias.astype(jnp.float32)).astype(jnp.bfloat16)
    project = jnp.einsum("rtd,de->rte", hidden1, w_qkv, preferred_element_type=jnp.float32)
    queries = ((project[..., :width] + query_bias.astype(jnp.float32)) * query_scale).astype(
        jnp.bfloat16
    )
    keys_own = project[..., width : 2 * width].astype(jnp.bfloat16)
    values_own = (project[..., 2 * width :] + value_bias.astype(jnp.float32)).astype(jnp.bfloat16)
    keys_all, values_all, segments_all = (
        lax.all_gather(keys_own, "tm", axis=1, tiled=True),
        lax.all_gather(values_own, "tm", axis=1, tiled=True),
        lax.all_gather(segment_ids, "tm", axis=1, tiled=True),
    )
    same = segment_ids[:, :, None] == segments_all[:, None, :]
    query_heads = split_heads(queries)
    head_outputs, log_totals = attend_forward(
        query_heads, split_heads(keys_all), split_heads(values_all), same
    )
    attended = join_heads(head_outputs).astype(jnp.bfloat16)
    middle = (
        inputs
        + jnp.einsum("rtd,de->rte", attended, w_out, preferred_element_type=jnp.float32)
        + out_bias.astype(jnp.float32)
    )
    normed2, inverse2 = normalize(middle)
    hidden2 = (normed2 * gain_two + norm2_bias.astype(jnp.float32)).astype(jnp.bfloat16)
    upper = jnp.einsum(
        "rtd,df->rtf", hidden2, w_up, preferred_element_type=jnp.float32
    ) + up_bias.astype(jnp.float32)
    activated = jax.nn.gelu(upper, approximate=False).astype(jnp.bfloat16)
    result = (
        middle
        + jnp.einsum("rtf,fd->rtd", activated, w_down, preferred_element_type=jnp.float32)
        + down_bias.astype(jnp.float32)
    )
    output = result.astype(jnp.bfloat16)
    grad_result = cotangent.astype(jnp.float32)
    grad_w_down = jnp.einsum(
        "rtf,rtd->fd", activated, cotangent, preferred_element_type=jnp.float32
    )
    grad_down_bias = total_rows(grad_result)
    grad_activated = jnp.einsum(
        "rtd,fd->rtf", cotangent, w_down, preferred_element_type=jnp.float32
    )
    unused, gelu_pull = jax.vjp(partial(jax.nn.gelu, approximate=False), upper)
    grad_upper = gelu_pull(grad_activated)[0].astype(jnp.bfloat16)
    grad_w_up = jnp.einsum("rtd,rtf->df", hidden2, grad_upper, preferred_element_type=jnp.float32)
    grad_up_bias = total_rows(grad_upper)
    grad_hidden2 = jnp.einsum("rtf,df->rtd", grad_upper, w_up, preferred_element_type=jnp.float32)
    grad_gain_two = total_rows(grad_hidden2 * normed2)
    grad_bias_two = total_rows(grad_hidden2)
    grad_middle = grad_result + norm_back(grad_hidden2, normed2, inverse2, gain_two)
    mlp_vectors = jnp.stack([grad_gain_two, grad_bias_two, grad_down_bias], axis=1)
    grad_branch = grad_middle.astype(jnp.bfloat16)
    grad_w_out = jnp.einsum(
        "rtd,rte->de", attended, grad_branch, preferred_element_type=jnp.float32
    )
    grad_out_bias = total_rows(grad_branch)
    grad_attended = jnp.einsum(
        "rte,de->rtd", grad_branch, w_out, preferred_element_type=jnp.float32
    ).astype(jnp.bfloat16)
    keys_back, values_back, segments_back = (
        lax.all_gather(keys_own, "tm", axis=1, tiled=True),
        lax.all_gather(values_own, "tm", axis=1, tiled=True),
        lax.all_gather(segment_ids, "tm", axis=1, tiled=True),
    )
    same_back = segment_ids[:, :, None] == segments_back[:, None, :]
    grad_query_h, grad_keys_h, grad_values_h = attend_backward(
        query_heads,
        split_heads(keys_back),
        split_heads(values_back),
        split_heads(grad_attended),
        log_totals,
        same_back,
    )
    grad_keys, grad_values = (
        lax.psum_scatter(
            join_heads(grad_keys_h).astype(jnp.bfloat16), "tm", scatter_dimension=1, tiled=True
        ).astype(jnp.float32),
        lax.psum_scatter(
            join_heads(grad_values_h).astype(jnp.bfloat16), "tm", scatter_dimension=1, tiled=True
        ).astype(jnp.float32),
    )
    grad_queries = join_heads(grad_query_h).astype(jnp.bfloat16)
    grad_project = jnp.concatenate(
        [
            (grad_queries.astype(jnp.float32) * query_scale).astype(jnp.bfloat16),
            grad_keys.astype(jnp.bfloat16),
            grad_values.astype(jnp.bfloat16),
        ],
        axis=-1,
    )
    grad_w_qkv = jnp.einsum(
        "rtd,rte->de", hidden1, grad_project, preferred_element_type=jnp.float32
    )
    grad_query_bias = total_rows(grad_project[..., :width])
    grad_value_bias = total_rows(grad_project[..., 2 * width :])
    grad_hidden1 = jnp.einsum(
        "rte,de->rtd", grad_project, w_qkv, preferred_element_type=jnp.float32
    )
    grad_gain_one = total_rows(grad_hidden1 * normed1)
    grad_bias_one = total_rows(grad_hidden1)
    grad_inputs = grad_middle + norm_back(grad_hidden1, normed1, inverse1, gain_one)
    grad_mask = total_rows(jnp.where(masked, grad_inputs, 0.0))
    grad_patches = jnp.where(masked, 0.0, grad_inputs).astype(jnp.bfloat16)
    attn_vectors = jnp.stack(
        [grad_mask, grad_gain_one, grad_bias_one, grad_query_bias, grad_value_bias, grad_out_bias],
        axis=1,
    )
    every_part = (
        lax.psum_scatter(
            grad_w_qkv.astype(jnp.bfloat16), "tm", scatter_dimension=0, tiled=True
        ).astype(jnp.float32),
        lax.psum_scatter(
            grad_w_out.astype(jnp.bfloat16), "tm", scatter_dimension=0, tiled=True
        ).astype(jnp.float32),
        lax.psum_scatter(
            attn_vectors.astype(jnp.bfloat16), "tm", scatter_dimension=0, tiled=True
        ).astype(jnp.float32),
        lax.psum_scatter(
            grad_w_up.astype(jnp.bfloat16), "tm", scatter_dimension=0, tiled=True
        ).astype(jnp.float32),
        lax.psum_scatter(
            grad_w_down.astype(jnp.bfloat16), "tm", scatter_dimension=0, tiled=True
        ).astype(jnp.float32),
        lax.psum_scatter(
            mlp_vectors.astype(jnp.bfloat16), "tm", scatter_dimension=0, tiled=True
        ).astype(jnp.float32),
        lax.psum_scatter(
            grad_up_bias.astype(jnp.bfloat16), "tm", scatter_dimension=0, tiled=True
        ).astype(jnp.float32),
    )
    every_part = (
        lax.psum(every_part[0].astype(jnp.bfloat16), "rows").astype(jnp.float32),
        lax.psum(every_part[1].astype(jnp.bfloat16), "rows").astype(jnp.float32),
        lax.psum(every_part[2].astype(jnp.bfloat16), "rows").astype(jnp.float32),
        lax.psum(every_part[3].astype(jnp.bfloat16), "rows").astype(jnp.float32),
        lax.psum(every_part[4].astype(jnp.bfloat16), "rows").astype(jnp.float32),
        lax.psum(every_part[5].astype(jnp.bfloat16), "rows").astype(jnp.float32),
        lax.psum(every_part[6].astype(jnp.bfloat16), "rows").astype(jnp.float32),
    )
    summed_qkv, summed_out, summed_attn, summed_up, summed_down, summed_mlp, summed_up_bias = (
        every_part
    )
    return (
        output,
        grad_patches,
        summed_attn[:, 0],
        summed_attn[:, 1],
        summed_attn[:, 2],
        summed_qkv,
        summed_attn[:, 3],
        summed_attn[:, 4],
        summed_out,
        summed_attn[:, 5],
        summed_mlp[:, 0],
        summed_mlp[:, 1],
        summed_up,
        summed_up_bias,
        summed_down,
        summed_mlp[:, 2],
    )


def solution(mesh):
    placed = (
        P("rows", "tm", None),
        P("rows", "tm"),
        P("rows", None),
        P(),
        P(),
        P(),
        P(),
        P(),
        P(),
        P(),
        P(),
        P(),
        P(),
        P(),
        P(),
        P(),
        P(),
        P("rows", "tm", None),
    )
    return jax.shard_map(
        shards,
        mesh=mesh,
        in_specs=placed,
        out_specs=(
            P("rows", "tm", None),
            P("rows", "tm", None),
            P("tm"),
            P("tm"),
            P("tm"),
            P("tm", None),
            P("tm"),
            P("tm"),
            P("tm", None),
            P("tm"),
            P("tm"),
            P("tm"),
            P("tm", None),
            P("tm"),
            P("tm", None),
            P("tm"),
        ),
        check_vma=False,
    )
```

profile of v0, /device:TPU:0, one launch (start us, length us, event | category | flops | bytes accessed | tf_op | source)
XLA Modules:
  0.0 761.7 jit_solution(18325670322503915509)
XLA Ops:
  32.9 5.7 all_gather.12
  38.5 12.7 %all-gather.5.cloned.1.call-done = bf16[1,1024,768]{2,1,0:T(8,128)(2,1)} async-done(((bf16[1,512,768]{2,1,0:T(8,128)(2,1)}), bf16[1,1024,768]{2,1,0:T(8,128)(2,1)}) %all-gather.5.cloned.1.call-update) | async-done | bytes 1572880 | tf_op jit(solution)/shard_map/all_gather | solution.py:130
  53.8 4.1 copy.65
  57.9 22.7 %all-gather.3.cloned.1.call-done = bf16[1,1024,768]{2,1,0:T(8,128)(2,1)} async-done(((bf16[1,512,768]{2,1,0:T(8,128)(2,1)}), bf16[1,1024,768]{2,1,0:T(8,128)(2,1)}) %all-gather.3.cloned.1.call-update) | async-done | bytes 1572880 | tf_op jit(solution)/shard_map/all_gather | solution.py:129
  83.1 4.1 copy.64
  88.2 57.6 %while.28 = (s32[]{:T(128)}, bf16[12,1,512,64]{2,3,1,0:T(8,128)(2,1)}, f32[12,1,512]{2,1,0:T(1,128)}, bf16[12,1,512,64]{3,2,1,0:T(8,128)(2,1)}, bf16[12,1,1024,6...) while((s32[]{:T(128)}, ...), condition=%wide.region_6.7_spmd.clone, body=%wide.region_3.6_spmd.clone.sunk | while | flops 137887232 | bytes 7105117 | solution.py:57
  149.1 20.5 %multiply_convert_fusion.1 = (bf16[512,3072]{1,0:T(8,128)(2,1)}, f32[512,3072]{1,0:T(8,128)}, f32[512,3072]{1,0:T(8,128)}) fusion(f32[3072]{0:T(1024)S(1)} %copy-done.22, bf16[768,3072]{1,0:T(8,128)(2,1)} %param.35, f32[1,512,768]{2,1,0:T(8,128)S(1)} %get-tuple-element.294, f32[768]{0:T(1024)S(1)} %copy-done.30, f32[768]{0:T(1024)S(1)} %copy-done.11, ...), kind=kOutput, calls=%fused_computation.52 | convolution fusion | flops 2521694208 | bytes 22042624 | tf_op jit(solution)/shard_map/rtd,df->rtf/dot_general | solution.py:146
  169.5 8.5 %fusion.87 = (bf16[3072]{0:T(1024)(128)(2,1)}, bf16[512,3072]{1,0:T(8,128)(2,1)S(1)}) fusion(f32[512,3072]{1,0:T(8,128)} %get-tuple-element.285, bf16[3072,768]{1,0:T(8,128)(2,1)S(1)} %bitcast.233, bf16[1,512,768]{2,1,0:T(8,128)(2,1)S(1)} %copy-done.8, f32[512,3072]{1,0:T(8,128)} %get-tuple-element.295, f32[3072]{0:T(1024)S(1)} %copy-done.22), kind=kOutput, calls=%fused_computation.151 | convolution fusion | flops 2441081856 | bytes 21252096 | tf_op jit(solution)/shard_map/rtd,fd->rtf/dot_general | solution.py:161
  189.8 117.3 %while.29 = (s32[]{:T(128)}, bf16[12,1,512,64]{2,3,1,0:T(8,128)(2,1)}, bf16[12,1,1024,64]{2,3,1,0:T(8,128)(2,1)}, bf16[12,1,1024,64]{2,3,1,0:T(8,128)(2,1)}, bf1...) while((s32[]{:T(128)}, ...), condition=%wide.region_13.14_spmd.clone, body=%wide.region_11.13_spmd.clone.sunk | while | flops 340262400 | bytes 17585272 | solution.py:83
  311.3 7.9 %convolution_convert_fusion.1 = bf16[768,3072]{1,0:T(8,128)(2,1)} fusion(bf16[512,3072]{1,0:T(8,128)(2,1)} %copy-done.35, f32[1,512,768]{2,1,0:T(8,128)} %copy-done.4, f32[768]{0:T(1024)} %convert_element_type.258, f32[768]{0:T(1024)S(1)} %copy-done.12, f32[512]{0:T(512)} %copy-done.27, f32[512]{0:T(512)S(1)} %copy-done.17), kind=kOutput, calls=%fused_computation.67 | convolution fusion | flops 2420244480 | bytes 9447424 | tf_op jit(solution)/shard_map/rtd,rtf->df/dot_general | solution.py:166
  319.5 7.0 convolution_convert_fusion
  329.4 4.1 reduce-scatter.13.cloned.1.call-done
  333.5 28.3 %reduce-scatter.15.cloned.1.call-done = bf16[1,512,768]{1,2,0:T(8,128)(2,1)} async-done(((bf16[1,1024,768]{1,2,0:T(8,128)(2,1)}), bf16[1,512,768]{1,2,0:T(8,128)(2,1)}) %reduce-scatter.15.cloned.1.call-update) | async-done | bytes 786448 | tf_op jit(solution)/shard_map/reduce_scatter | solution.py:199
  361.8 6.1 convolution_convert_fusion.2
  372.9 4.5 fusion.48
  386.3 62.9 %reduce-scatter.21.cloned.1.call-done = bf16[384,3072]{1,0:T(8,128)(2,1)} async-done(((bf16[768,3072]{1,0:T(8,128)(2,1)}), bf16[384,3072]{1,0:T(8,128)(2,1)}) %reduce-scatter.21.cloned.1.call-update) | async-done | bytes 2359312 | tf_op jit(solution)/shard_map/reduce_scatter | solution.py:239
  449.1 63.0 %reduce-scatter.23.cloned.1.call-done = bf16[1536,768]{1,0:T(8,128)(2,1)} async-done(((bf16[3072,768]{1,0:T(8,128)(2,1)}), bf16[1536,768]{1,0:T(8,128)(2,1)}) %reduce-scatter.23.cloned.1.call-update) | async-done | bytes 2359312 | tf_op jit(solution)/shard_map/reduce_scatter | solution.py:242
  512.1 50.6 %reduce-scatter.17.cloned.1.call-done = bf16[384,2304]{1,0:T(8,128)(2,1)} async-done(((bf16[768,2304]{1,0:T(8,128)(2,1)}), bf16[384,2304]{1,0:T(8,128)(2,1)}) %reduce-scatter.17.cloned.1.call-update) | async-done | bytes 1769488 | tf_op jit(solution)/shard_map/reduce_scatter | solution.py:230
  565.2 5.0 all-reduce
  570.3 7.2 fusion.56
  580.7 8.4 %reduce-scatter.25.cloned.1.call-done = bf16[384,6]{1,0:T(8,128)(2,1)} async-done(((bf16[768,6]{1,0:T(8,128)(2,1)}), bf16[384,6]{1,0:T(8,128)(2,1)}) %reduce-scatter.25.cloned.1.call-update) | async-done | bytes 4624
  590.1 63.7 %all-reduce.1 = (bf16[384,6]{0,1:T(8,128)(2,1)}, bf16[384,3]{0,1:T(4,128)(2,1)}, bf16[1536]{0:T(1024)(128)(2,1)}) all-reduce(bf16[384,6]{0,1:T(8,128)(2,1)S(1)} %copy.72, bf16[384,3]{0,1:T(4,128)(2,1)S(1)} %copy.74, bf16[1536]{0:T(1024)(128)(2,1)S(1)} %dynamic-slice.1), channel_id=1, replica_groups=mesh['rows'=16,'tm'=2] {'rows'}, use_global_device_ids=true, to_apply=%region_25.26 | all-reduce | flops 4992 | bytes 19968 | tf_op jit(solution)/shard_map/psum | solution.py:255
  657.6 86.8 %all-reduce.5.cloned.1.call-done = (bf16[384,2304]{1,0:T(8,128)(2,1)}, bf16[384,768]{1,0:T(8,128)(2,1)}, bf16[384,3072]{1,0:T(8,128)(2,1)}, bf16[1536,768]{1,0:T(8,128)(2,1)}) async-done(((bf16[384,2304]{1,0:T(8,128)(2,1)}, bf16[384,768]{1,0:T(8,128)(2,1)}, bf16[384,3072]{1,0:T(8,128)(2,1)}, bf16[1536,768]{1,0:T(8,128)(2,1)}), (bf16[384,2304]{1,0:T(8,128)(2,1)}, bf16[384,768]{1,0:T(8,128)(2,1)}, ...) | async-done | bytes 7077904 | tf_op jit(solution)/shard_map/psum | solution.py:253
  744.5 4.6 convert_element_type.288
  (321 shorter events, 257.9 us)
Async XLA Ops:
  7.2 44.0 %all-gather.5.cloned.1.call-start = ((), (), s32[]{:S(2)}) async-start(), calls=%async_computation.9 | async-start | bytes 2359296 | tf_op jit(solution)/shard_map/all_gather | solution.py:130
  9.1 9.3 %copy-start.18 = (pred[512]{0:T(512)(128)(4,1)}, pred[512]{0:T(512)(128)(4,1)S(1)}, u32[]{:S(2)}) copy-start(pred[512]{0:T(512)(128)(4,1)S(1)} %compare_reduce_fusion) | copy-start | bytes 1540
  21.1 59.4 %all-gather.3.cloned.1.call-start = ((), (), s32[]{:S(2)}) async-start(), calls=%async_computation.8 | async-start | bytes 2359296 | tf_op jit(solution)/shard_map/all_gather | solution.py:129
  23.6 9.3 %copy-start.10 = (s32[1,512]{1,0:T(1,128)S(1)}, s32[1,512]{1,0:T(1,128)}, u32[]{:S(2)}) copy-start(s32[1,512]{1,0:T(1,128)} %param.23) | copy-start | bytes 6148
  23.6 309.9 %reduce-scatter.13.cloned.1.call-start = ((), (), s32[]{:S(2)}) async-start(), calls=%async_computation.10 | async-start | bytes 2359296 | tf_op jit(solution)/shard_map/reduce_scatter | solution.py:196
  145.8 23.8 %slice-start.2 = ((s8[4718592]{0:T(1024)(128)(4,1)}), s8[4194304]{0:T(1024)(128)(4,1)S(1)}, s32[]{:S(2)}) async-start(s8[4718592]{0:T(1024)(128)(4,1)} %bitcast.232), calls=%async_computation.21 | async-start | bytes 8388608
  145.8 32.3 %slice-start = ((s8[4718592]{0:T(1024)(128)(4,1)}), s8[4194304]{0:T(1024)(128)(4,1)S(1)}, s32[]{:S(2)}) async-start(s8[4718592]{0:T(1024)(128)(4,1)} %bitcast.230), calls=%async_computation.19 | async-start | bytes 8388608
  148.6 33.6 %copy-start.4 = (f32[1,512,768]{2,1,0:T(8,128)}, f32[1,512,768]{2,1,0:T(8,128)S(1)}, u32[]{:S(2)}) copy-start(f32[1,512,768]{2,1,0:T(8,128)S(1)} %get-tuple-element.294) | copy-start | bytes 4718596
  148.7 33.5 %copy-start.16 = (f32[512]{0:T(512)}, f32[512]{0:T(512)S(1)}, u32[]{:S(2)}) copy-start(f32[512]{0:T(512)S(1)} %broadcast_multiply_fusion.4) | copy-start | bytes 6148
  149.0 33.2 %copy-start.27 = (f32[512]{0:T(512)}, f32[512]{0:T(512)S(1)}, u32[]{:S(2)}) copy-start(f32[512]{0:T(512)S(1)} %add_rsqrt_fusion) | copy-start | bytes 6148
  149.0 20.5 %copy-start.8 = (bf16[1,512,768]{2,1,0:T(8,128)(2,1)S(1)}, bf16[1,512,768]{2,1,0:T(8,128)(2,1)}, u32[]{:S(2)}) copy-start(bf16[1,512,768]{2,1,0:T(8,128)(2,1)} %param.39) | copy-start | bytes 2359300
  149.0 20.5 %slice-start.3 = ((s8[4718592]{0:T(1024)(128)(4,1)}), s8[524288]{0:T(1024)(128)(4,1)S(1)}, s32[]{:S(2)}) async-start(s8[4718592]{0:T(1024)(128)(4,1)} %bitcast.232), calls=%async_computation.22 | async-start | bytes 1048576
  149.1 29.0 %slice-start.1 = ((s8[4718592]{0:T(1024)(128)(4,1)}), s8[524288]{0:T(1024)(128)(4,1)S(1)}, s32[]{:S(2)}) async-start(s8[4718592]{0:T(1024)(128)(4,1)} %bitcast.230), calls=%async_computation.20 | async-start | bytes 1048576
  307.1 54.6 %reduce-scatter.15.cloned.1.call-start = ((), (), s32[]{:S(2)}) async-start(), calls=%async_computation.11 | async-start | bytes 2359296 | tf_op jit(solution)/shard_map/reduce_scatter | solution.py:199
  307.8 78.5 %reduce-scatter.19.cloned.1.call-start = ((), (), s32[]{:S(2)}) async-start(), calls=%async_computation.13 | async-start | bytes 1769472 | tf_op jit(solution)/shard_map/reduce_scatter | solution.py:233
  311.3 137.8 %reduce-scatter.21.cloned.1.call-start = ((), (), s32[]{:S(2)}) async-start(), calls=%async_computation.14 | async-start | bytes 7077888 | tf_op jit(solution)/shard_map/reduce_scatter | solution.py:239
  319.2 192.8 %reduce-scatter.23.cloned.1.call-start = ((), (), s32[]{:S(2)}) async-start(), calls=%async_computation.15 | async-start | bytes 7077888 | tf_op jit(solution)/shard_map/reduce_scatter | solution.py:242
  326.5 35.2 %copy-start.14 = (f32[512]{0:T(512)S(1)}, f32[512]{0:T(512)}, u32[]{:S(2)}) copy-start(f32[512]{0:T(512)} %copy-done.13) | copy-start | bytes 6148
  326.5 35.2 %copy-start.19 = (pred[512]{0:T(512)(128)(4,1)S(1)}, pred[512]{0:T(512)(128)(4,1)}, u32[]{:S(2)}) copy-start(pred[512]{0:T(512)(128)(4,1)} %copy-done.18) | copy-start | bytes 1540
  326.6 236.1 %reduce-scatter.17.cloned.1.call-start = ((), (), s32[]{:S(2)}) async-start(), calls=%async_computation.12 | async-start | bytes 5308416 | tf_op jit(solution)/shard_map/reduce_scatter | solution.py:230
  367.9 209.6 %reduce-scatter.27.cloned.1.call-start = ((), (), s32[]{:S(2)}) async-start(), calls=%async_computation.17 | async-start | bytes 294912
  372.8 216.3 %reduce-scatter.25.cloned.1.call-start = ((), (), s32[]{:S(2)}) async-start(), calls=%async_computation.16 | async-start | bytes 294912
  385.1 359.4 %all-reduce.5.cloned.1.call-start = ((), (), s32[]{:S(2)}) async-start(), calls=%async_computation.18 | async-start | bytes 14155776 | tf_op jit(solution)/shard_map/psum | solution.py:253
  570.3 8.2 %copy-start.21 = (pred[512]{0:T(512)(128)(4,1)S(1)}, pred[512]{0:T(512)(128)(4,1)}, u32[]{:S(2)}) copy-start(pred[512]{0:T(512)(128)(4,1)} %copy-done.18) | copy-start | bytes 1540
  (27 other events, 94.1 us)
Sparse Core Ops, SparseCore 0:
  21.2 29.9 all-gather.4
  53.3 27.1 all-gather.2
  307.3 26.1 reduce-scatter.12
  335.6 26.1 reduce-scatter.14
  364.4 21.8 reduce-scatter.18
  389.0 60.0 reduce-scatter.20
  452.0 60.0 reduce-scatter.22
  514.9 47.7 reduce-scatter.16
  564.9 11.0 reduce-scatter.26
  578.0 11.0 reduce-scatter.24
  593.2 151.2 all-reduce.4
where the time goes:
time: 769 us; the launch traced here: 762 us
  waiting for transfers between devices  341 us (44%)
  matrix products  227 us (30%)
  blocking collectives  74.3 us (10%)
  local copies, waits for them, and re-layouts  55.8 us (7%)
  other arithmetic  47.3 us (6%)
  between operations  15.4 us (2%)
    psum x1, waiting for transfers between devices, shards(): lax.psum(every_part[0].astype(jnp.bfloat16), 'rows').astype(jnp.float32)  86.8 us
    psum x1, blocking collectives, shards(): lax.psum(every_part[2].astype(jnp.bfloat16), 'rows').astype(jnp.float32)  63.7 us
    reduce_scatter x1, waiting for transfers between devices, shards(): lax.psum_scatter(grad_w_down.astype(jnp.bfloat16), 'tm', scatter_dimensio...  63 us
    reduce_scatter x1, waiting for transfers between devices, shards(): lax.psum_scatter(grad_w_up.astype(jnp.bfloat16), 'tm', scatter_dimension=...  62.9 us
    reduce_scatter x1, waiting for transfers between devices, shards(): lax.psum_scatter(grad_w_qkv.astype(jnp.bfloat16), 'tm', scatter_dimension...  50.6 us
    dot_general x24, matrix products, head_scores(): jnp.einsum('rqd,rkd->rqk', query, keys_h, preferred_element_type=jnp.floa...  37.2 us
    reduce_scatter x1, waiting for transfers between devices, shards(): lax.psum_scatter(join_heads(grad_values_h).astype(jnp.bfloat16), 'tm', sc...  28.3 us
    dot_general x12, matrix products, one_head(): jnp.einsum('rqk,rkd->rqd', weights, values_h, preferred_element_type=jnp....  25.7 us
  transfers between devices with their start and end apart: 11, of which 10 were waited for; matrix products, arithmetic and copies ran while one was open for 10% of the time, Pallas kernels for 0%

commit v1 on v0

--- a/solution.py
+++ b/solution.py
@@ -4,6 +4,8 @@
 import jax
 import jax.numpy as jnp
 from jax import lax
+from jax.experimental import pallas as pl
+from jax.experimental.pallas import tpu as pltpu
 from jax.sharding import PartitionSpec as P
 
 HEADS = 12
@@ -83,11 +85,202 @@
     return lax.map(one_head, (query_heads, key_heads, value_heads, grad_heads, log_totals))
 
 
+MESH = pl.DeviceIdType.MESH
+SUB = 96
+COLS = 384
+LAGS = (0, 1, 3, 4, 5, 7, 8, 9)
+
+
+def places():
+    row = lax.axis_index("rows")
+    y = lax.axis_index("tm")
+    core = row % 2
+    x = (row // 2) % 2
+    z_low = (row // 4) % 2
+    z_high = row // 8
+    peers = (
+        (row + 1 - 2 * core, y),
+        (row, 1 - y),
+        (row + 2 - 4 * x, y),
+        (row + 4 - 8 * z_low, y),
+        (row + 8 - 16 * z_high, y),
+    )
+    return core, x, y, peers
+
+
+def greet(peers):
+    barrier = pltpu.get_barrier_semaphore()
+    for peer in peers:
+        pl.semaphore_signal(barrier, inc=1, device_id=peer, device_id_type=MESH)
+    pl.semaphore_wait(barrier, len(peers))
+
+
+def reduce_kernel(
+    count, g_ref, vec_ref, out_ref, vec_out, r1, r2, r3, r4, r5, done, v1, v2, ssem, rsem, vs, vr
+):
+    core, x, y, peers = places()
+    pair, yp, xp, zp1, zp2 = peers
+    greet(peers)
+
+    def copy(s, c):
+        src, dst, dev = (
+            lambda: (g_ref.at[c, 1 - core], r1.at[c], pair),
+            lambda: (r1.at[c, 1 - y], r2.at[c], yp),
+            lambda: (r2.at[c, 1 - x], r3.at[c], xp),
+            lambda: (r3.at[c], r4.at[c], zp1),
+            lambda: (r4.at[c], r5.at[c], zp2),
+            lambda: (done.at[c, core, x], done.at[c, core, x], xp),
+            lambda: (done.at[c, core], done.at[c, core], pair),
+        )[s]()
+        return pltpu.make_async_remote_copy(
+            src_ref=src,
+            dst_ref=dst,
+            send_sem=ssem.at[s, c],
+            recv_sem=rsem.at[s, c],
+            device_id=dev,
+            device_id_type=MESH,
+        )
+
+    def stage(s, c):
+        if s > 0:
+            copy(s - 1, c).wait_recv()
+        if s == 1:
+            r1[c] = r1[c] + g_ref[c, core]
+        elif s == 2:
+            r2[c] = r2[c] + r1[c, y]
+        elif s == 3:
+            r3[c] = r3[c] + r2[c, x]
+        elif s == 4:
+            r4[c] = r4[c] + r3[c]
+        elif s == 5:
+            done[c, core, x] = r5[c] + r4[c]
+        elif s == 7:
+            out_ref[c] = done[c]
+        if s < 7:
+            copy(s, c).start()
+
+    def vec_copy(s):
+        src, dst, dev = (
+            lambda: (vec_ref, v1, pair),
+            lambda: (v1.at[1 - y], v2.at[0], yp),
+            lambda: (v2.at[0], v2.at[1], xp),
+            lambda: (v2.at[1], v2.at[2], zp1),
+            lambda: (v2.at[2], v2.at[3], zp2),
+        )[s]()
+        return pltpu.make_async_remote_copy(
+            src_ref=src,
+            dst_ref=dst,
+            send_sem=vs.at[s],
+            recv_sem=vr.at[s],
+            device_id=dev,
+            device_id_type=MESH,
+        )
+
+    def vec_stage(s):
+        if s > 0:
+            vec_copy(s - 1).wait_recv()
+        if s == 1:
+            v1[...] = v1[...] + vec_ref[...]
+        elif s == 2:
+            v2[0] = v2[0] + v1[y]
+        elif s == 5:
+            vec_out[...] = v2[3] + v2[2]
+        elif s > 2:
+            v2[s - 2] = v2[s - 2] + v2[s - 3]
+        if s < 5:
+            vec_copy(s).start()
+
+    def step(t, carry):
+        for s in range(8):
+            c = t - LAGS[s]
+
+            @pl.when((c >= 0) & (c < count))
+            def _():
+                stage(s, c)
+
+        for s in range(6):
+
+            @pl.when(t == 2 * s)
+            def _():
+                vec_stage(s)
+
+        return carry
+
+    lax.fori_loop(0, count + LAGS[7], step, 0)
+
+    def drain(c, carry):
+        for s in range(7):
+            copy(s, c).wait_send()
+        return carry
+
+    lax.fori_loop(0, count, drain, 0)
+    for s in range(5):
+        vec_copy(s).wait_send()
+
+
+def reduce_gradients(chunks, vectors):
+    count = chunks.shape[0]
+    rows_v = vectors.shape[1]
+
+    def low(*shape):
+        return pltpu.VMEM(shape, jnp.bfloat16)
+
+    return pl.pallas_call(
+        partial(reduce_kernel, count),
+        out_shape=(
+            jax.ShapeDtypeStruct((count, 2, 2, SUB, COLS), jnp.bfloat16),
+            jax.ShapeDtypeStruct((rows_v, COLS), jnp.float32),
+        ),
+        in_specs=[pl.BlockSpec(memory_space=pltpu.VMEM)] * 2,
+        out_specs=(pl.BlockSpec(memory_space=pltpu.VMEM),) * 2,
+        scratch_shapes=[
+            low(count, 2, 2, SUB, COLS),
+            low(count, 2, SUB, COLS),
+            low(count, SUB, COLS),
+            low(count, SUB, COLS),
+            low(count, SUB, COLS),
+            low(count, 2, 2, SUB, COLS),
+            pltpu.VMEM((2, rows_v, COLS), jnp.float32),
+            pltpu.VMEM((4, rows_v, COLS), jnp.float32),
+            pltpu.SemaphoreType.DMA((7, count)),
+            pltpu.SemaphoreType.DMA((7, count)),
+            pltpu.SemaphoreType.DMA((5,)),
+            pltpu.SemaphoreType.DMA((5,)),
+        ],
+        compiler_params=pltpu.CompilerParams(
+            collective_id=0, has_side_effects=True, vmem_limit_bytes=62 << 20
+        ),
+    )(chunks, vectors)
+
+
+def wide_chunks(grad):
+    n = grad.shape[1] // COLS
+    return grad.reshape(2, 2, 2, SUB, n, COLS).transpose(4, 1, 0, 2, 3, 5)
+
+
+def tall_chunks(grad):
+    n = grad.shape[0] // 768
+    blocks = grad.reshape(2, n, 2, 2, SUB, 2, COLS).transpose(1, 5, 2, 0, 3, 4, 6)
+    return blocks.reshape(2 * n, 2, 2, 2, SUB, COLS)
+
+
+def wide_whole(part):
+    n = part.shape[0]
+    return part.reshape(n, 384, COLS).transpose(1, 0, 2).reshape(384, n * COLS).astype(jnp.float32)
+
+
+def tall_whole(part):
+    n = part.shape[0] // 2
+    blocks = part.reshape(n, 2, 384, COLS).transpose(0, 2, 1, 3)
+    return blocks.reshape(n * 384, 768).astype(jnp.float32)
+
+
 def total_rows(tensor):
     return jnp.sum(tensor.astype(jnp.float32), axis=(0, 1))
 
 
 def shards(
+    block,
     patches,
     segment_ids,
     mask_positions,
@@ -226,6 +419,38 @@
         [grad_mask, grad_gain_one, grad_bias_one, grad_query_bias, grad_value_bias, grad_out_bias],
         axis=1,
     )
+    if block:
+        chunks = jnp.concatenate(
+            [
+                wide_chunks(grad_w_up.astype(jnp.bfloat16)),
+                tall_chunks(grad_w_down.astype(jnp.bfloat16)),
+                wide_chunks(grad_w_out.astype(jnp.bfloat16)),
+                wide_chunks(grad_w_qkv.astype(jnp.bfloat16)),
+            ]
+        )
+        vectors = jnp.concatenate(
+            [attn_vectors.T, mlp_vectors.T, jnp.zeros((3, width), jnp.float32)]
+        ).reshape(12, 2, 384)
+        vectors = jnp.concatenate([vectors[:9].transpose(1, 0, 2), grad_up_bias.reshape(2, 4, 384), vectors[9:].transpose(1, 0, 2)], axis=1)
+        parts, v = reduce_gradients(chunks, vectors)
+        return (
+            output,
+            grad_patches,
+            v[0],
+            v[1],
+            v[2],
+            wide_whole(parts[18:]),
+            v[3],
+            v[4],
+            wide_whole(parts[16:18]),
+            v[5],
+            v[6],
+            v[7],
+            wide_whole(parts[:8]),
+            v[9:13].reshape(-1),
+            tall_whole(parts[8:16]),
+            v[8],
+        )
     every_part = (
         lax.psum_scatter(
             grad_w_qkv.astype(jnp.bfloat16), "tm", scatter_dimension=0, tiled=True
@@ -303,7 +528,7 @@
         P("rows", "tm", None),
     )
     return jax.shard_map(
-        shards,
+        partial(shards, dict(mesh.shape) == {"rows": 16, "tm": 2}),
         mesh=mesh,
         in_specs=placed,
         out_specs=(

time: 769 us -> 555 us (0.72)
  waiting for transfers between devices: 341 us -> 44.5 us
  Pallas kernels: 0 us -> 114 us
  blocking collectives: 74.3 us -> 5.49 us
  local copies, waits for them, and re-layouts: 55.8 us -> 106 us
  matrix products: 227 us -> 212 us
    reduce_scatter x4 -> x0, waiting for transfers between devices: 178 us -> none  [the longest x1 63 us: shards(): lax.psum_scatter(grad_w_down.astype(jnp.bfloat16), 'tm', scatter_dimensio...]
    pallas_call x0 -> x1, Pallas kernels: none -> 114 us  [reduce_gradients(): pl.pallas_call(partial(reduce_kernel, count), out_shape=(jax.ShapeDtypeSt...]
    psum x1 -> x0, waiting for transfers between devices: 86.8 us -> none  [shards(): lax.psum(every_part[0].astype(jnp.bfloat16), 'rows').astype(jnp.float32)]
    psum x1 -> x0, blocking collectives: 63.7 us -> none  [shards(): lax.psum(every_part[2].astype(jnp.bfloat16), 'rows').astype(jnp.float32)]
    reshape x0 -> x9, local copies, waits for them, and re-layouts: none -> 37 us  [the longest x5 19.3 us: wide_chunks(): return grad.reshape(2, 2, 2, SUB, n, COLS).transpose(4, 1, 0, 2, 3, 5)]
    reduce_scatter x1, waiting for transfers between devices: 28.3 us -> 0.01 us  [shards(): lax.psum_scatter(join_heads(grad_values_h).astype(jnp.bfloat16), 'tm', sc...]
    concatenate x0 -> x3, other arithmetic: none -> 14.5 us  [the longest x1 12.4 us: shards(): jnp.concatenate([wide_chunks(grad_w_up.astype(jnp.bfloat16)), tall_chunks...]
    convert_element_type x0 -> x4, local copies, waits for them, and re-layouts: none -> 12.7 us  [the longest x3 9.06 us: wide_whole(): part.reshape(n, 384, COLS).transpose(1, 0, 2).reshape(384, n * COLS)]
  transfers between devices with their start and end apart: 11 -> 4, of which waited for: 10 -> 3; matrix products, arithmetic and copies ran while one was open for 10% -> 12% of each run, Pallas kernels for 0% -> 0%
where the time goes in v1:
time: 555 us; the launch traced here: 546 us
  matrix products  212 us (38%)
  Pallas kernels  114 us (21%)
  local copies, waits for them, and re-layouts  106 us (19%)
  other arithmetic  50 us (9%)
  waiting for transfers between devices  44.5 us (8%)
  between operations  14.8 us (3%)
    pallas_call x1, Pallas kernels, reduce_gradients(): pl.pallas_call(partial(reduce_kernel, count), out_shape=(jax.ShapeDtypeSt...  114 us
    dot_general x24, matrix products, head_scores(): jnp.einsum('rqd,rkd->rqk', query, keys_h, preferred_element_type=jnp.floa...  37.3 us
    all_gather x1, waiting for transfers between devices, shards(): lax.all_gather(values_own, 'tm', axis=1, tiled=True)  24.9 us
    dot_general x12, matrix products, one_head(): jnp.einsum('rqk,rkd->rqd', grad_scores, keys_h, preferred_element_type=jn...  24.4 us
    dot_general x12, matrix products, one_head(): jnp.einsum('rqk,rqd->rkd', grad_scores, query, preferred_element_type=jnp...  22.7 us
    dot_general x12, matrix products, one_head(): jnp.einsum('rqk,rqd->rkd', probs_low, grad_out, preferred_element_type=jn...  21.5 us
    dot_general x1, matrix products, shards(): jnp.einsum('rtd,df->rtf', hidden2, w_up, preferred_element_type=jnp.float32)  20.8 us
    reshape x5, local copies, waits for them, and re-layouts, wide_chunks(): return grad.reshape(2, 2, 2, SUB, n, COLS).transpose(4, 1, 0, 2, 3, 5)  19.3 us
  transfers between devices with their start and end apart: 4, of which 3 were waited for; matrix products, arithmetic and copies ran while one was open for 12% of the time, Pallas kernels for 0%

profile of v1, /device:TPU:0, one launch (start us, length us, event | category | flops | bytes accessed | tf_op | source)
XLA Modules:
  0.0 546.3 jit_solution(11201629787973657954)
XLA Ops:
  13.4 4.5 convolution_bitcast_fusion.4
  28.0 5.5 %all_gather.12 = s32[1,1024]{1,0:T(1,128)S(1)} all-gather(s32[1,512]{1,0:T(1,128)S(1)} %copy-done.16), channel_id=1, replica_groups=mesh['rows'=16,'tm'=2] {'tm'}, dimensions={1}, use_global_device_ids=true | all-gather | bytes 6144 | tf_op jit(solution)/shard_map/all_gather | solution.py:324
  33.5 17.7 %all-gather.3.cloned.1.call-done = bf16[1,1024,768]{2,1,0:T(8,128)(2,1)} async-done(((bf16[1,512,768]{2,1,0:T(8,128)(2,1)}), bf16[1,1024,768]{2,1,0:T(8,128)(2,1)}) %all-gather.3.cloned.1.call-update) | async-done | bytes 1572880 | tf_op jit(solution)/shard_map/all_gather | solution.py:322
  55.6 24.9 %all-gather.5.cloned.1.call-done = bf16[1,1024,768]{2,1,0:T(8,128)(2,1)} async-done(((bf16[1,512,768]{2,1,0:T(8,128)(2,1)}), bf16[1,1024,768]{2,1,0:T(8,128)(2,1)}) %all-gather.5.cloned.1.call-update) | async-done | bytes 1572880 | tf_op jit(solution)/shard_map/all_gather | solution.py:323
  85.1 50.1 %while.28 = (s32[]{:T(128)}, bf16[12,1,512,64]{2,3,1,0:T(8,128)(2,1)S(1)}, f32[12,1,512]{2,1,0:T(1,128)}, bf16[12,1,512,64]{3,2,1,0:T(8,128)(2,1)}, bf16[12,1,10...) while((s32[]{:T(128)}, ...), condition=%wide.region_6.7_spmd.clone, body=%wide.region_3.6_spmd.clone.sunk | while | flops 137887232 | bytes 7104617 | solution.py:59
  136.6 20.8 %multiply_convert_fusion.1 = (bf16[512,3072]{1,0:T(8,128)(2,1)}, f32[512,3072]{1,0:T(8,128)}, f32[512,3072]{1,0:T(8,128)}) fusion(f32[3072]{0:T(1024)S(1)} %copy-done.33, bf16[768,3072]{1,0:T(8,128)(2,1)} %param.35, f32[1,512,768]{2,1,0:T(8,128)S(1)} %get-tuple-element.306, f32[768]{0:T(1024)S(1)} %copy-done.45, f32[768]{0:T(1024)S(1)} %convert_element_type.270, ...), kind=kOutput, calls=%fused_computation.54 | convolution fusion | flops 2521694208 | bytes 22042624 | tf_op jit(solution)/shard_map/rtd,df->rtf/dot_general | solution.py:339
  157.4 8.4 %convert_reduce_fusion = (f32[3072]{0:T(1024)}, bf16[512,3072]{1,0:T(8,128)(2,1)S(1)}) fusion(f32[512,3072]{1,0:T(8,128)} %get-tuple-element.295, bf16[3072,768]{1,0:T(8,128)(2,1)S(1)} %bitcast.292, bf16[1,512,768]{2,1,0:T(8,128)(2,1)S(1)} %copy-done.11, f32[512,3072]{1,0:T(8,128)} %get-tuple-element.307, f32[3072]{0:T(1024)S(1)} %copy-done.33), kind=kOutput, calls=%fused_computation.52 | convolution fusion | flops 2442654720 | bytes 21258240 | tf_op jit(solution)/shard_map/rtd,fd->rtf/dot_general | solution.py:354
  165.8 3.4 fusion.47
  176.3 117.1 %while.29 = (s32[]{:T(128)}, bf16[12,1,512,64]{2,3,1,0:T(8,128)(2,1)}, bf16[12,1,1024,64]{2,3,1,0:T(8,128)(2,1)}, bf16[12,1,1024,64]{2,3,1,0:T(8,128)(2,1)}, bf1...) while((s32[]{:T(128)}, ...), condition=%wide.region_13.14_spmd.clone, body=%wide.region_11.13_spmd.clone.sunk | while | flops 340262400 | bytes 17585280 | solution.py:85
  300.6 6.7 %convolution_convert_fusion.1 = bf16[3072,768]{1,0:T(8,128)(2,1)} fusion(bf16[512,3072]{1,0:T(8,128)(2,1)} %get-tuple-element.294, bf16[1,512,768]{2,1,0:T(8,128)(2,1)S(1)} %copy-done.12), kind=kOutput, calls=%fused_computation.69 | convolution fusion | flops 2418278400 | bytes 8650752 | tf_op jit(solution)/shard_map/rtf,rtd->fd/dot_general | solution.py:350
  307.4 10.1 %reshape.647 = bf16[2,4,2,2,96,2,384]{6,5,4,3,2,1,0:T(2,128)(2,1)} reshape(bf16[3072,768]{1,0:T(8,128)(2,1)} %convolution_convert_fusion.1) | data formatting | bytes 9437184 | tf_op jit(solution)/shard_map/reshape | solution.py:263
  317.5 5.7 %copy.76 = bf16[2,4,2,2,96,2,384]{6,4,3,0,2,5,1:T(8,128)(2,1)} copy(bf16[2,4,2,2,96,2,384]{6,5,4,3,2,1,0:T(2,128)(2,1)} %reshape.647) | data formatting | bytes 9437184 | tf_op jit(solution)/shard_map/reshape | solution.py:263
  323.2 3.4 convolution_convert_fusion.2
  339.4 7.2 %fusion.55 = bf16[1,512,768]{2,1,0:T(8,128)(2,1)} fusion(f32[1,512,768]{2,1,0:T(8,128)} %copy-done.4, bf16[512,3072]{1,0:T(8,128)(2,1)} %get-tuple-element.294, bf16[3072,768]{1,0:T(8,128)(2,1)} %param.37, f32[768]{0:T(1024)} %convert_element_type.275), kind=kOutput, calls=%fused_computation.101 | convolution fusion | flops 2417098752 | bytes 10226688 | tf_op jit(solution)/shard_map/rtf,fd->rtd/dot_general | solution.py:345
  348.0 6.2 %fusion.48 = (f32[768]{0:T(1024)}, f32[512]{0:T(512)S(1)}, f32[512,768]{1,0:T(8,128)S(1)}) fusion(bf16[1,512,768]{2,1,0:T(8,128)(2,1)S(1)} %copy-done.3, f32[512]{0:T(512)} %copy-done.34, f32[512]{0:T(512)S(1)} %copy-done.20, f32[768]{0:T(1024)S(1)} %convert_element_type.257, pred[512]{0:T(512)(128)(4,1)S(1)} %copy-done.29, f32[768]{0:T(1024)S(1)} %copy-done.18, ...), kind=kOutput, calls=%fused_computation.89 | convolution fusion | flops 1822554880 | bytes 8273408 | tf_op jit(solution)/shard_map/rte,de->rtd/dot_general | solution.py:410
  356.2 4.3 convolution_convert_fusion
  360.5 7.9 %reshape.650 = bf16[2,2,2,96,6,384]{5,4,3,2,1,0:T(8,128)(2,1)} reshape(bf16[768,2304]{1,0:T(8,128)(2,1)} %convolution_convert_fusion) | data formatting | bytes 7077888 | tf_op jit(solution)/shard_map/reshape | solution.py:258
  368.4 4.9 copy.95
  378.2 12.4 %pad_maximum_fusion.g_ref = bf16[24,2,2,2,96,384]{5,4,3,2,1,0:T(8,128)(2,1)} fusion(bf16[6,2,2,2,96,384]{5,4,3,2,1,0:T(8,128)(2,1)} %bitcast.266, bf16[2,2,2,2,96,384]{5,4,3,2,1,0:T(8,128)(2,1)S(1)} %bitcast.270, bf16[8,2,2,2,96,384]{5,4,3,2,1,0:T(8,128)(2,1)} %bitcast.261, bf16[8,2,2,2,96,384]{5,4,3,2,1,0:T(8,128)(2,1)} %bitcast.262), kind=kLoop, calls=%fused_computation.49 | loop fusion | flops 21233664 | bytes 28311552 | tf_op jit(solution)/shard_map/concatenate | solution.py:423
  390.6 113.6 %shard_map.300 = (bf16[24,2,2,96,384]{4,3,2,1,0:T(8,128)(2,1)}, f32[16,384]{1,0:T(8,128)}) custom-call(bf16[24,2,2,2,96,384]{5,4,3,2,1,0:T(8,128)(2,1)} %pad_maximum_fusion.g_ref, f32[2,16,384]{2,1,0:T(8,128)} %maximum_maximum_fusion.vec_ref), custom_call_target="tpu_custom_call" | custom-call | tf_op jit(solution)/shard_map/pallas_call | solution.py:228
  507.8 4.5 fusion.84
  516.2 5.2 copy.80
  521.4 5.3 copy.84
  533.4 3.6 copy.83
  (358 shorter events, 245.1 us)
Async XLA Ops:
  7.2 128.0 %copy-start = (bf16[768,768]{1,0:T(8,128)(2,1)S(1)}, bf16[768,768]{1,0:T(8,128)(2,1)}, u32[]{:S(2)}) copy-start(bf16[768,768]{1,0:T(8,128)(2,1)} %param.31) | copy-start | bytes 3538948
  7.2 44.0 %all-gather.3.cloned.1.call-start = ((), (), s32[]{:S(2)}) async-start(), calls=%async_computation.2 | async-start | bytes 2359296 | tf_op jit(solution)/shard_map/all_gather | solution.py:322
  8.0 9.9 %copy-start.43 = (f32[768]{0:T(1024)}, f32[768]{0:T(1024)S(1)}, u32[]{:S(2)}) copy-start(f32[768]{0:T(1024)S(1)} %convert_element_type.260) | copy-start | bytes 9220
  8.7 9.2 %copy-start.17 = (f32[768]{0:T(1024)}, f32[768]{0:T(1024)S(1)}, u32[]{:S(2)}) copy-start(f32[768]{0:T(1024)S(1)} %convert_element_type.259) | copy-start | bytes 9220
  21.1 59.4 %all-gather.5.cloned.1.call-start = ((), (), s32[]{:S(2)}) async-start(), calls=%async_computation.3 | async-start | bytes 2359296 | tf_op jit(solution)/shard_map/all_gather | solution.py:323
  24.3 322.4 %reduce-scatter.5.cloned.1.call-start = ((), (), s32[]{:S(2)}) async-start(), calls=%async_computation.5 | async-start | bytes 2359296 | tf_op jit(solution)/shard_map/reduce_scatter | solution.py:392
  85.1 50.1 %copy-start.3 = (bf16[1,512,768]{2,1,0:T(8,128)(2,1)S(1)}, bf16[1,512,768]{2,1,0:T(8,128)(2,1)}, u32[]{:S(2)}) copy-start(bf16[1,512,768]{2,1,0:T(8,128)(2,1)} %param.22) | copy-start | bytes 2359300
  85.1 50.1 %copy-start.28 = (pred[512]{0:T(512)(128)(4,1)S(1)}, pred[512]{0:T(512)(128)(4,1)}, u32[]{:S(2)}) copy-start(pred[512]{0:T(512)(128)(4,1)} %copy-done.27) | copy-start | bytes 1540
  85.1 50.1 %copy-start.47 = (f32[768]{0:T(1024)S(1)}, f32[768]{0:T(1024)}, u32[]{:S(2)}) copy-start(f32[768]{0:T(1024)} %convert_element_type.269) | copy-start | bytes 9220
  135.2 22.2 %slice-start.2 = ((s8[4718592]{0:T(1024)(128)(4,1)}), s8[4194304]{0:T(1024)(128)(4,1)S(1)}, s32[]{:S(2)}) async-start(s8[4718592]{0:T(1024)(128)(4,1)} %bitcast.291), calls=%async_computation.8 | async-start | bytes 8388608
  135.2 30.6 %slice-start = ((s8[4718592]{0:T(1024)(128)(4,1)}), s8[4194304]{0:T(1024)(128)(4,1)S(1)}, s32[]{:S(2)}) async-start(s8[4718592]{0:T(1024)(128)(4,1)} %bitcast.289), calls=%async_computation.6 | async-start | bytes 8388608
  136.2 33.8 %copy-start.4 = (f32[1,512,768]{2,1,0:T(8,128)}, f32[1,512,768]{2,1,0:T(8,128)S(1)}, u32[]{:S(2)}) copy-start(f32[1,512,768]{2,1,0:T(8,128)S(1)} %get-tuple-element.306) | copy-start | bytes 4718596
  136.2 33.8 %copy-start.21 = (f32[512]{0:T(512)}, f32[512]{0:T(512)S(1)}, u32[]{:S(2)}) copy-start(f32[512]{0:T(512)S(1)} %broadcast_multiply_fusion.4) | copy-start | bytes 6148
  136.6 33.4 %copy-start.37 = (f32[512]{0:T(512)}, f32[512]{0:T(512)S(1)}, u32[]{:S(2)}) copy-start(f32[512]{0:T(512)S(1)} %add_rsqrt_fusion) | copy-start | bytes 6148
  136.6 20.8 %copy-start.11 = (bf16[1,512,768]{2,1,0:T(8,128)(2,1)S(1)}, bf16[1,512,768]{2,1,0:T(8,128)(2,1)}, u32[]{:S(2)}) copy-start(bf16[1,512,768]{2,1,0:T(8,128)(2,1)} %param.39) | copy-start | bytes 2359300
  136.6 20.8 %slice-start.3 = ((s8[4718592]{0:T(1024)(128)(4,1)}), s8[524288]{0:T(1024)(128)(4,1)S(1)}, s32[]{:S(2)}) async-start(s8[4718592]{0:T(1024)(128)(4,1)} %bitcast.291), calls=%async_computation.9 | async-start | bytes 1048576
  136.6 29.2 %slice-start.1 = ((s8[4718592]{0:T(1024)(128)(4,1)}), s8[524288]{0:T(1024)(128)(4,1)S(1)}, s32[]{:S(2)}) async-start(s8[4718592]{0:T(1024)(128)(4,1)} %bitcast.289), calls=%async_computation.7 | async-start | bytes 1048576
  293.4 54.6 %reduce-scatter.3.cloned.1.call-start = ((), (), s32[]{:S(2)}) async-start(), calls=%async_computation.4 | async-start | bytes 2359296 | tf_op jit(solution)/shard_map/reduce_scatter | solution.py:389
  327.8 9.7 %copy-start.23 = (f32[768]{0:T(1024)S(1)}, f32[768]{0:T(1024)}, u32[]{:S(2)}) copy-start(f32[768]{0:T(1024)} %get-tuple-element.288) | copy-start | bytes 9220
  339.4 8.5 %copy-start.18 = (f32[768]{0:T(1024)S(1)}, f32[768]{0:T(1024)}, u32[]{:S(2)}) copy-start(f32[768]{0:T(1024)} %copy-done.17) | copy-start | bytes 9220
  339.4 8.5 %copy-start.20 = (f32[512]{0:T(512)S(1)}, f32[512]{0:T(512)}, u32[]{:S(2)}) copy-start(f32[512]{0:T(512)} %copy-done.19) | copy-start | bytes 6148
  339.4 8.5 %copy-start.29 = (pred[512]{0:T(512)(128)(4,1)S(1)}, pred[512]{0:T(512)(128)(4,1)}, u32[]{:S(2)}) copy-start(pred[512]{0:T(512)(128)(4,1)} %copy-done.27) | copy-start | bytes 1540
  347.9 8.2 %copy-start.13 = (bf16[1,512,768]{1,2,0:T(8,128)(2,1)S(1)}, bf16[1,512,768]{1,2,0:T(8,128)(2,1)}, u32[]{:S(2)}) copy-start(bf16[1,512,768]{1,2,0:T(8,128)(2,1)} %reduce-scatter.5.cloned.1.call-done) | copy-start | bytes 2359300
  348.0 8.2 %copy-start.15 = (bf16[12,1,512,64]{2,3,1,0:T(8,128)(2,1)S(1)}, bf16[12,1,512,64]{2,3,1,0:T(8,128)(2,1)}, u32[]{:S(2)}) copy-start(bf16[12,1,512,64]{2,3,1,0:T(8,128)(2,1)} %get-tuple-element.291) | copy-start | bytes 2359300
  (41 other events, 168.5 us)
Sparse Core Ops, SparseCore 0:
  21.3 29.9 all-gather.2
  53.3 27.1 all-gather.4
  293.5 26.1 reduce-scatter.4
  321.8 26.1 reduce-scatter.2
